TPU v7x, 32 devices: a whole 2x2x4 slice. The times are simulated.
32 devices in a mesh: row: 4 (over y, core), col: 8 (over z, x).
Axes of the slice: x: 2, y: 2, z: 4, core: 2. Of those that a mesh axis runs over, the one named last changes fastest.
Arguments:
- calib: bfloat16 [256, 8192], replicated, may hold values from -6 to 6
- gate_a: bfloat16 [8192, 28672], P('col', 'row'), may hold values from -0.0625 to 0.0625
- up_a: bfloat16 [8192, 28672], P('col', 'row'), may hold values from -0.0625 to 0.0625
- gate_b: bfloat16 [8192, 28672], P('row', 'col'), may hold values from -0.0625 to 0.0625
- up_b: bfloat16 [8192, 28672], P('row', 'col'), may hold values from -0.0625 to 0.0625
- down_a: bfloat16 [28672, 1024], P(('row', 'col')), may hold values from -6 to 6
- down_b: bfloat16 [28672, 1024], P('col', 'row'), may hold values from -6 to 6
Outputs:
- joined: bfloat16 [28672, 1024], P(('row', 'col'))
All inputs are finite; a program needn't handle non-finite values.
Results may differ from a plain program's by a relative error of at most 0.025.
Values may be sent and summed in bfloat16 or wider, within the bound.
A program may use at most 384 MiB of HBM per device.

v0:
```python
import jax
import jax.numpy as jnp
from jax import lax
from jax.sharding import PartitionSpec as P

ITERS = 3


softness = 0.02
statistic_floor = 1e-05


def standardize(gate_pre, up_preactivation):
    hidden = jax.nn.silu(gate_pre) * up_preactivation
    center = jnp.mean(hidden, axis=0, keepdims=True)
    spread = jnp.mean(jnp.square(hidden - center), axis=0, keepdims=True)
    return ((hidden - center) * lax.rsqrt(spread + statistic_floor)).astype(jnp.bfloat16)


def per_device(calib, gate_a, up_a, gate_b, up_b, down_a, down_b):
    width_a = gate_a.shape[0]
    width_b = gate_b.shape[0]
    inputs_a = lax.dynamic_slice_in_dim(calib, lax.axis_index("col") * width_a, width_a, 1)
    inputs_b = lax.dynamic_slice_in_dim(calib, lax.axis_index("row") * width_b, width_b, 1)
    gate_pre_a = jnp.dot(inputs_a, gate_a, preferred_element_type=jnp.float32)
    up_pre_a = jnp.dot(inputs_a, up_a, preferred_element_type=jnp.float32)
    gate_pre_b = jnp.dot(inputs_b, gate_b, preferred_element_type=jnp.float32)
    up_pre_b = jnp.dot(inputs_b, up_b, preferred_element_type=jnp.float32)
    complete_first_gate, whole_up_a = lax.psum((gate_pre_a, up_pre_a), "col")
    first_model_scores = standardize(complete_first_gate, whole_up_a)
    whole_gate_b, whole_up_b = (
        lax.psum(gate_pre_b.astype(jnp.bfloat16), "row").astype(jnp.float32),
        lax.psum(up_pre_b.astype(jnp.bfloat16), "row").astype(jnp.float32),
    )
    scores_b = standardize(whole_gate_b, whole_up_b)
    multiplier = 1.0 / (calib.shape[0] * softness)
    logits = lax.dot_general(
        first_model_scores, scores_b, (((0,), (0,)), ((), ())), preferred_element_type=jnp.float32
    )
    kernel = jnp.exp(logits * multiplier)
    column_scaling = jnp.ones((kernel.shape[1],), jnp.float32)
    for step in range(ITERS):
        row_part = jnp.dot(kernel, column_scaling, precision=lax.Precision.HIGHEST)
        row_scale = 1.0 / lax.psum(row_part, "col")
        col_part = jnp.dot(row_scale, kernel, precision=lax.Precision.HIGHEST)
        column_scaling = 1.0 / lax.psum(col_part, "row")
    rows_full = lax.all_gather(down_b, "row", axis=1, tiled=True)
    plan = (row_scale[:, None] * kernel * column_scaling[None, :]).astype(jnp.bfloat16)
    aligned = lax.psum_scatter(
        jnp.dot(plan, rows_full, preferred_element_type=jnp.float32).astype(jnp.bfloat16),
        "col",
        scatter_dimension=0,
        tiled=True,
    ).astype(jnp.float32)
    return ((down_a.astype(jnp.float32) + aligned) * 0.5).astype(jnp.bfloat16)


def solution(mesh):
    placed = (
        P(),
        P("col", "row"),
        P("col", "row"),
        P("row", "col"),
        P("row", "col"),
        P(("row", "col"), None),
        P("col", "row"),
    )
    return jax.shard_map(
        per_device, mesh=mesh, in_specs=placed, out_specs=P(("row", "col"), None), check_vma=False
    )
```

profile of v0, /device:TPU:0, one launch (start us, length us, event | category | flops | bytes accessed | tf_op | source)
XLA Modules:
  0.0 1489.8 jit_solution(903566750479565874)
XLA Ops:
  6.5 10.9 convolution_convert_fusion.1
  17.4 6.4 convolution_convert_fusion
  23.8 0.0 all-reduce.5.cloned.1.call-start
  23.9 12.4 fusion.16
  36.4 7.2 fusion.14
  43.6 0.0 all-gather.2.cloned.1.call-start
  43.6 0.7 all-gather.2.cloned.1.call-update
  44.3 0.3 reduce-scatter.2.cloned.1.call-start
  44.6 59.1 %all-reduce.7.cloned.1.call-done = (bf16[256,3584]{1,0:T(8,128)(2,1)}, bf16[256,3584]{1,0:T(8,128)(2,1)}) async-done(((bf16[256,3584]{1,0:T(8,128)(2,1)}, bf16[256,3584]{1,0:T(8,128)(2,1)}), (bf16[256,3584]{1,0:T(8,128)(2,1)}, bf16[256,3584]{1,0:T(8,128)(2,1)})) %all-reduce.7.cloned.1.call-update) | async-done | bytes 3670032 | tf_op jit(solution)/shard_map/psum | solution.py:33
  103.7 3.2 fusion.26
  106.9 3.4 multiply_reduce_fusion.1
  110.4 452.6 %all-reduce.5.cloned.1.call-done = (f32[256,7168]{1,0:T(8,128)}, f32[256,7168]{1,0:T(8,128)}) async-done(((f32[256,7168]{1,0:T(8,128)}, f32[256,7168]{1,0:T(8,128)}), (f32[256,7168]{1,0:T(8,128)}, f32[256,7168]{1,0:T(8,128)})) %all-reduce.5.cloned.1.call-update) | async-done | bytes 14680080 | tf_op jit(solution)/shard_map/psum | solution.py:29
  562.9 6.3 fusion.27
  569.2 3.9 copy-done
  573.1 0.8 multiply_reduce_fusion
  574.0 40.8 %multiply_exponential_fusion = f32[7168,3584]{1,0:T(8,128)} fusion(f32[256,7168]{1,0:T(8,128)} %copy-done, f32[7168]{0:T(1024)S(1)} %add_rsqrt_fusion, f32[7168]{0:T(1024)S(1)} %broadcast_multiply_fusion, f32[3584]{0:T(1024)S(1)} %add_rsqrt_fusion.1, f32[3584]{0:T(1024)S(1)} %broadcast_multiply_fusion.1, bf16[256,3584]{1,0:T(8,128)(2,1)} %get-tuple-element.8, ...), kind=kOutput, calls=%fused_computation.1 | convolution fusion | flops 13193707520 | bytes 113856512 | tf_op jit(solution)/shard_map/dot_general | solution.py:37
  614.8 90.8 %fusion.18 = f32[1,7168]{1,0:T(1,128)S(1)} fusion(f32[7168,3584]{1,0:T(8,128)} %multiply_exponential_fusion), kind=kOutput, calls=%fused_computation.43 | convolution fusion | flops 308281344 | bytes 102789120 | tf_op jit(solution)/shard_map/dot_general | solution.py:43
  705.6 34.8 %psum.74 = f32[7168]{0:T(1024)S(1)} all-reduce(f32[7168]{0:T(1024)S(1)} %bitcast.30), channel_id=1, replica_groups=mesh['row'=4,'col'=8] {'col'}, use_global_device_ids=true, to_apply=%region_8.9 | all-reduce | flops 7168 | bytes 57344 | tf_op jit(solution)/shard_map/psum | solution.py:44
  740.4 54.0 %convolution_reduce_fusion.2 = f32[3584]{0:T(1024)S(1)} fusion(f32[7168,1]{0,1:T(1,128)S(1)} %bitcast.26, f32[7168,3584]{1,0:T(8,128)} %multiply_exponential_fusion), kind=kOutput, calls=%fused_computation.26 | convolution fusion | flops 308281344 | bytes 102803456 | tf_op jit(solution)/shard_map/dot_general | solution.py:45
  794.4 10.3 psum.75
  804.7 90.7 %fusion.28 = f32[1,7168]{1,0:T(1,128)S(1)} fusion(f32[7168,3584]{1,0:T(8,128)} %multiply_exponential_fusion, f32[3584,1]{0,1:T(1,128)S(1)} %reshape.30), kind=kOutput, calls=%fused_computation.52 | convolution fusion | flops 308281344 | bytes 102803456 | tf_op jit(solution)/shard_map/dot_general | solution.py:43
  895.4 33.3 %psum.76 = f32[7168]{0:T(1024)S(1)} all-reduce(f32[7168]{0:T(1024)S(1)} %bitcast.28), channel_id=1, replica_groups=mesh['row'=4,'col'=8] {'col'}, use_global_device_ids=true, to_apply=%region_10.11 | all-reduce | flops 7168 | bytes 57344 | tf_op jit(solution)/shard_map/psum | solution.py:44
  928.7 54.0 %convolution_reduce_fusion.1 = f32[3584]{0:T(1024)S(1)} fusion(f32[7168,1]{0,1:T(1,128)S(1)} %bitcast.27, f32[7168,3584]{1,0:T(8,128)} %multiply_exponential_fusion), kind=kOutput, calls=%fused_computation.25 | convolution fusion | flops 308281344 | bytes 102803456 | tf_op jit(solution)/shard_map/dot_general | solution.py:45
  982.7 10.4 psum.77
  993.1 90.7 %fusion.29 = f32[1,7168]{1,0:T(1,128)S(1)} fusion(f32[7168,3584]{1,0:T(8,128)} %multiply_exponential_fusion, f32[3584,1]{0,1:T(1,128)S(1)} %reshape.34), kind=kOutput, calls=%fused_computation.53 | convolution fusion | flops 308281344 | bytes 102803456 | tf_op jit(solution)/shard_map/dot_general | solution.py:43
  1083.8 33.4 %psum.78 = f32[7168]{0:T(1024)S(1)} all-reduce(f32[7168]{0:T(1024)S(1)} %bitcast.29), channel_id=1, replica_groups=mesh['row'=4,'col'=8] {'col'}, use_global_device_ids=true, to_apply=%region_12.13 | all-reduce | flops 7168 | bytes 57344 | tf_op jit(solution)/shard_map/psum | solution.py:44
  1117.1 54.0 %convolution_reduce_fusion = f32[3584]{0:T(1024)S(1)} fusion(f32[7168,1]{0,1:T(1,128)S(1)} %bitcast.25, f32[7168,3584]{1,0:T(8,128)} %multiply_exponential_fusion), kind=kOutput, calls=%fused_computation.24 | convolution fusion | flops 308281344 | bytes 102803456 | tf_op jit(solution)/shard_map/dot_general | solution.py:45
  1171.1 10.4 psum.79
  1181.6 0.0 all-gather.2.cloned.1.call-done
  1181.6 63.1 %fusion.3 = bf16[7168,1024]{1,0:T(8,128)(2,1)} fusion(bf16[3584,1024]{1,0:T(8,128)(2,1)} %all-gather.2.cloned.1.call-done, f32[7168,3584]{1,0:T(8,128)} %multiply_exponential_fusion, f32[3584]{0:T(1024)S(1)} %broadcast_divide_fusion.5, f32[7168]{0:T(1024)S(1)} %broadcast_divide_fusion), kind=kOutput, calls=%fused_computation.5 | convolution fusion | flops 52697759744 | bytes 124823552 | tf_op jit(solution)/shard_map/dot_general | solution.py:50
  1244.7 234.4 %reduce-scatter.2.cloned.1.call-done = bf16[896,1024]{1,0:T(8,128)(2,1)} async-done(((bf16[7168,1024]{1,0:T(8,128)(2,1)}), bf16[896,1024]{1,0:T(8,128)(2,1)}) %reduce-scatter.2.cloned.1.call-update) | async-done | bytes 1835024 | tf_op jit(solution)/shard_map/reduce_scatter | solution.py:49
  1479.1 3.5 multiply_convert_fusion.6
  (32 shorter events, 0.2 us)
Async XLA Ops:
  6.5 97.2 %all-reduce.7.cloned.1.call-start = ((), (), s32[]{:S(2)}) async-start(), calls=%async_computation.4 | async-start | bytes 7340032 | tf_op jit(solution)/shard_map/psum | solution.py:33
  6.5 10.9 copy-start.3
  23.8 12.5 slice-start
  23.8 539.1 %all-reduce.5.cloned.1.call-start = ((), (), s32[]{:S(2)}) async-start(), calls=%async_computation.3 | async-start | bytes 29360128 | tf_op jit(solution)/shard_map/psum | solution.py:29
  23.9 12.5 slice-start.1
  23.9 12.4 slice-start.2
  23.9 12.4 slice-start.3
  43.6 1138.0 %all-gather.2.cloned.1.call-start = ((), (), s32[]{:S(2)}) async-start(), calls=%async_computation.1 | async-start | bytes 9175040 | tf_op jit(solution)/shard_map/all_gather | solution.py:47
  44.3 1434.8 %reduce-scatter.2.cloned.1.call-start = ((), (), s32[]{:S(2)}) async-start(), calls=%async_computation.2 | async-start | bytes 16515072 | tf_op jit(solution)/shard_map/reduce_scatter | solution.py:49
  569.2 4.0 copy-start
  569.2 4.8 copy-start.1
  1244.7 234.4 %copy-start.2 = (bf16[896,1024]{1,0:T(8,128)(2,1)S(1)}, bf16[896,1024]{1,0:T(8,128)(2,1)}, u32[]{:S(2)}) copy-start(bf16[896,1024]{1,0:T(8,128)(2,1)} %param.12) | copy-start | bytes 5505028
Sparse Core Ops, SparseCore 0:
  23.9 79.7 all-reduce.6
  108.0 454.8 all-reduce.4
  564.5 52.3 all-gather.1
  1244.9 234.2 reduce-scatter.1
where the time goes:
time: 1500 us; the launch traced here: 1490 us
  waiting for transfers between devices  747 us (50%)
  matrix products  575 us (38%)
  blocking collectives  133 us (9%)
  other arithmetic  17.4 us (1%)
    psum x1, waiting for transfers between devices, per_device(): complete_first_gate, whole_up_a = lax.psum((gate_pre_a, up_pre_a), 'col')  453 us
    dot_general x3, matrix products, per_device(): row_part = jnp.dot(kernel, column_scaling, precision=lax.Precision.HIGHEST)  272 us
    reduce_scatter x1, waiting for transfers between devices, per_device(): lax.psum_scatter(jnp.dot(plan, rows_full, preferred_element_type=jnp.floa...  234 us
    dot_general x3, matrix products, per_device(): col_part = jnp.dot(row_scale, kernel, precision=lax.Precision.HIGHEST)  162 us
    psum x3, blocking collectives, per_device(): row_scale = 1.0 / lax.psum(row_part, 'col')  101 us
    dot_general x1, matrix products, per_device(): jnp.dot(plan, rows_full, preferred_element_type=jnp.float32)  63.1 us
    psum x1, waiting for transfers between devices, per_device(): lax.psum(up_pre_b.astype(jnp.bfloat16), 'row').astype(jnp.float32)  59.1 us
    dot_general x1, matrix products, per_device(): lax.dot_general(first_model_scores, scores_b, (((0,), (0,)), ((), ())), p...  40.8 us
  transfers between devices with their start and end apart: 4, of which 3 were waited for; matrix products, arithmetic and copies ran while one was open for 34% of the time, Pallas kernels for 0%

commit v1 on v0

v1 whole, which is shorter than its diff:
```python
import jax
import jax.numpy as jnp
from jax import lax
from jax.experimental import pallas as pl
from jax.experimental.pallas import tpu as pltpu
from jax.sharding import PartitionSpec as P

ITERS = 3


softness = 0.02
statistic_floor = 1e-05
LANES = 128


def standardize(gate_pre, up_preactivation):
    hidden = jax.nn.silu(gate_pre) * up_preactivation
    center = jnp.mean(hidden, axis=0, keepdims=True)
    spread = jnp.mean(jnp.square(hidden - center), axis=0, keepdims=True)
    return ((hidden - center) * lax.rsqrt(spread + statistic_floor)).astype(jnp.bfloat16)


def block_of(size, most):
    block = most
    while size % block:
        block //= 2
    return block


def lane_chunk(size, most):
    chunk = most
    while size % chunk:
        chunk -= LANES
    return chunk


def make_kernel(scores_a, scores_b, multiplier):
    rows, depth = scores_a.shape
    cols = scores_b.shape[0]
    block = block_of(rows, 512)
    chunk = lane_chunk(cols, 512)

    def body(a_ref, b_ref, k_ref, s_ref):
        total = jnp.zeros((block, LANES), jnp.float32)
        for start in range(0, cols, chunk):
            logits = lax.dot_general(
                a_ref[...], b_ref[start : start + chunk, :], (((1,), (1,)), ((), ())),
                preferred_element_type=jnp.float32,
            )
            values = jnp.exp(logits * multiplier)
            k_ref[:, start : start + chunk] = values.astype(jnp.bfloat16)
            for lane in range(0, chunk, LANES):
                total = total + values[:, lane : lane + LANES]
        s_ref[...] = jnp.sum(total, axis=1, keepdims=True)

    return pl.pallas_call(
        body,
        grid=(rows // block,),
        in_specs=[
            pl.BlockSpec((block, depth), lambda i: (i, 0)),
            pl.BlockSpec((cols, depth), lambda i: (0, 0)),
        ],
        out_specs=[
            pl.BlockSpec((block, cols), lambda i: (i, 0)),
            pl.BlockSpec((block, 1), lambda i: (i, 0)),
        ],
        out_shape=[
            jax.ShapeDtypeStruct((rows, cols), jnp.bfloat16),
            jax.ShapeDtypeStruct((rows, 1), jnp.float32),
        ],
        cost_estimate=pl.CostEstimate(
            flops=2 * rows * cols * depth, bytes_accessed=2 * rows * cols, transcendentals=rows * cols
        ),
        name="make_kernel",
    )(scores_a, scores_b)


def row_pass(kernel, column_scaling):
    rows, cols = kernel.shape
    block = block_of(rows, 512)
    group = block_of(block, 64)

    def body(k_ref, c_ref, s_ref):
        @pl.loop(0, block // group)
        def _(step):
            base = pl.multiple_of(step * group, group)
            total = jnp.zeros((group, LANES), jnp.float32)
            for lane in range(0, cols, LANES):
                total = total + (
                    k_ref[pl.ds(base, group), lane : lane + LANES].astype(jnp.float32)
                    * c_ref[:, lane : lane + LANES]
                )
            s_ref[pl.ds(base, group), :] = jnp.sum(total, axis=1, keepdims=True)

    return pl.pallas_call(
        body,
        grid=(rows // block,),
        in_specs=[
            pl.BlockSpec((block, cols), lambda i: (i, 0)),
            pl.BlockSpec((1, cols), lambda i: (0, 0)),
        ],
        out_specs=pl.BlockSpec((block, 1), lambda i: (i, 0)),
        out_shape=jax.ShapeDtypeStruct((rows, 1), jnp.float32),
        cost_estimate=pl.CostEstimate(
            flops=2 * rows * cols, bytes_accessed=2 * rows * cols, transcendentals=0
        ),
        name="row_pass",
    )(kernel, column_scaling)


def col_pass(kernel, row_scale):
    rows, cols = kernel.shape
    block = block_of(rows, 512)

    def body(k_ref, r_ref, s_ref):
        @pl.when(pl.program_id(0) == 0)
        def _():
            s_ref[...] = jnp.zeros_like(s_ref)

        for lane in range(0, cols, LANES):
            part = k_ref[:, lane : lane + LANES].astype(jnp.float32) * r_ref[...]
            s_ref[:, lane : lane + LANES] += jnp.sum(part, axis=0, keepdims=True)

    return pl.pallas_call(
        body,
        grid=(rows // block,),
        in_specs=[
            pl.BlockSpec((block, cols), lambda i: (i, 0)),
            pl.BlockSpec((block, LANES), lambda i: (i, 0)),
        ],
        out_specs=pl.BlockSpec((1, cols), lambda i: (0, 0)),
        out_shape=jax.ShapeDtypeStruct((1, cols), jnp.float32),
        cost_estimate=pl.CostEstimate(
            flops=2 * rows * cols, bytes_accessed=2 * rows * cols, transcendentals=0
        ),
        name="col_pass",
    )(kernel, jnp.broadcast_to(row_scale, (rows, LANES)))


def scores_of(gate_pre, up_pre, axis, parts, wire):
    tokens, width = gate_pre.shape
    own = width // parts
    both = jnp.stack((gate_pre.astype(wire), up_pre.astype(wire)))
    both = both.reshape(2, tokens, parts, own).transpose(2, 0, 1, 3)
    summed = lax.psum_scatter(both, axis, scatter_dimension=0, tiled=False).astype(jnp.float32)
    mine = standardize(summed[0], summed[1]).T
    return lax.all_gather(mine, axis, axis=0, tiled=True)


def solution(mesh):
    n_row, n_col = mesh.shape["row"], mesh.shape["col"]

    def per_device(calib, gate_a, up_a, gate_b, up_b, down_a, down_b):
        width_a = gate_a.shape[0]
        width_b = gate_b.shape[0]
        inputs_a = lax.dynamic_slice_in_dim(calib, lax.axis_index("col") * width_a, width_a, 1)
        inputs_b = lax.dynamic_slice_in_dim(calib, lax.axis_index("row") * width_b, width_b, 1)
        gate_pre_a = jnp.dot(inputs_a, gate_a, preferred_element_type=jnp.float32)
        up_pre_a = jnp.dot(inputs_a, up_a, preferred_element_type=jnp.float32)
        gate_pre_b = jnp.dot(inputs_b, gate_b, preferred_element_type=jnp.float32)
        up_pre_b = jnp.dot(inputs_b, up_b, preferred_element_type=jnp.float32)
        scores_a = scores_of(gate_pre_a, up_pre_a, "col", n_col, jnp.bfloat16)
        scores_b = scores_of(gate_pre_b, up_pre_b, "row", n_row, jnp.float32)
        rows_full = lax.all_gather(down_b, "row", axis=1, tiled=True)
        multiplier = 1.0 / (calib.shape[0] * softness)
        kernel, row_part = make_kernel(scores_a, scores_b, multiplier)
        for step in range(ITERS):
            if step:
                row_part = row_pass(kernel, column_scaling)
            row_scale = 1.0 / lax.psum(row_part[:, 0], "col")[:, None]
            column_scaling = 1.0 / lax.psum(col_pass(kernel, row_scale), "row")
        scaled = (rows_full.astype(jnp.float32) * column_scaling.reshape(-1, 1)).astype(jnp.bfloat16)
        window = scaled.shape[1]
        pieces = []
        for cut in range(0, window, window // 4):
            part = jnp.dot(kernel, scaled[:, cut : cut + window // 4], preferred_element_type=jnp.float32)
            part = (part * row_scale).astype(jnp.bfloat16)
            pieces.append(lax.psum_scatter(part, "col", scatter_dimension=0, tiled=True))
        aligned = jnp.concatenate(pieces, axis=1).astype(jnp.float32)
        return ((down_a.astype(jnp.float32) + aligned) * 0.5).astype(jnp.bfloat16)

    placed = (
        P(),
        P("col", "row"),
        P("col", "row"),
        P("row", "col"),
        P("row", "col"),
        P(("row", "col"), None),
        P("col", "row"),
    )
    return jax.shard_map(
        per_device, mesh=mesh, in_specs=placed, out_specs=P(("row", "col"), None), check_vma=False
    )
```

time: 1500 us -> 1030 us (0.69)
  matrix products: 575 us -> 137 us
  waiting for transfers between devices: 747 us -> 523 us
  Pallas kernels: 0 us -> 151 us
  local copies, waits for them, and re-layouts: 3.98 us -> 27.3 us
  other arithmetic: 17.4 us -> 36.7 us
    psum x2 -> x0, waiting for transfers between devices: 512 us -> none  [the longest x1 453 us: per_device(): complete_first_gate, whole_up_a = lax.psum((gate_pre_a, up_pre_a), 'col')]
    dot_general x8 -> x4, matrix products: 538 us -> 92 us  [per_device(): jnp.dot(kernel, scaled[:, cut:cut + window // 4], preferred_element_type=...]
    reduce_scatter x1 -> x6, waiting for transfers between devices: 234 us -> 435 us  [the longest x4 262 us: per_device(): lax.psum_scatter(part, 'col', scatter_dimension=0, tiled=True)]
    pallas_call x0 -> x6, Pallas kernels: none -> 151 us  [the longest x3 68.8 us: col_pass(): pl.pallas_call(body, grid=(rows // block,), in_specs=[pl.BlockSpec((block...]
    all_gather x0 -> x2, waiting for transfers between devices: none -> 87.2 us  [scores_of(): return lax.all_gather(mine, axis, axis=0, tiled=True)]
  transfers between devices with their start and end apart: 4 -> 9, of which waited for: 3 -> 8; matrix products, arithmetic and copies ran while one was open for 34% -> 12% of each run, Pallas kernels for 0% -> 15%
where the time goes in v1:
time: 1030 us; the launch traced here: 1020 us
  waiting for transfers between devices  523 us (51%)
  Pallas kernels  151 us (15%)
  matrix products  137 us (13%)
  blocking collectives  133 us (13%)
  other arithmetic  36.7 us (4%)
  local copies, waits for them, and re-layouts  27.3 us (3%)
  between operations  13.7 us (1%)
    reduce_scatter x4, waiting for transfers between devices, per_device(): lax.psum_scatter(part, 'col', scatter_dimension=0, tiled=True)  262 us
    reduce_scatter x2, waiting for transfers between devices, scores_of(): lax.psum_scatter(both, axis, scatter_dimension=0, tiled=False)  173 us
    psum x3, blocking collectives, per_device(): row_scale = 1.0 / lax.psum(row_part[:, 0], 'col')[:, None]  101 us
    dot_general x4, matrix products, per_device(): jnp.dot(kernel, scaled[:, cut:cut + window // 4], preferred_element_type=...  92 us
    all_gather x2, waiting for transfers between devices, scores_of(): return lax.all_gather(mine, axis, axis=0, tiled=True)  87.2 us
    pallas_call x3, Pallas kernels, col_pass(): pl.pallas_call(body, grid=(rows // block,), in_specs=[pl.BlockSpec((block...  68.8 us
    pallas_call x2, Pallas kernels, row_pass(): pl.pallas_call(body, grid=(rows // block,), in_specs=[pl.BlockSpec((block...  55.7 us
    psum x3, blocking collectives, per_device(): column_scaling = 1.0 / lax.psum(col_pass(kernel, row_scale), 'row')  32 us
  transfers between devices with their start and end apart: 9, of which 8 were waited for; matrix products, arithmetic and copies ran while one was open for 12% of the time, Pallas kernels for 15%

profile of v1, /device:TPU:0, one launch (start us, length us, event | category | flops | bytes accessed | tf_op | source)
XLA Modules:
  0.0 1022.6 jit_solution(7075433411296789035)
XLA Ops:
  6.5 11.1 %convolution_convert_fusion.1 = bf16[256,7168]{1,0:T(8,128)(2,1)} fusion(bf16[1024,7168]{1,0:T(8,128)(2,1)} %param.8, bf16[256,8192]{1,0:T(8,128)(2,1)} %param.7, s32[]{:T(128)S(6)} %select_n.6), kind=kOutput, calls=%fused_computation.10 | convolution fusion | flops 3759931392 | bytes 18874372 | tf_op jit(solution)/shard_map/dot_general | solution.py:158
  17.7 5.9 copy.12
  23.6 11.1 %convolution_convert_fusion = bf16[256,7168]{1,0:T(8,128)(2,1)} fusion(bf16[1024,7168]{1,0:T(8,128)(2,1)} %param.9, bf16[256,8192]{1,0:T(8,128)(2,1)} %param.7, s32[]{:T(128)S(6)} %select_n.6), kind=kOutput, calls=%fused_computation.9 | convolution fusion | flops 3759931392 | bytes 18874372 | tf_op jit(solution)/shard_map/dot_general | solution.py:159
  34.7 5.9 copy.13
  40.6 6.8 maximum_bitcast_fusion
  48.0 9.6 fusion.10
  57.5 13.2 %fusion.8 = f32[256,3584]{0,1:T(8,128)} fusion(bf16[2048,3584]{1,0:T(8,128)(2,1)} %param.11, bf16[256,8192]{1,0:T(8,128)(2,1)} %param.7, s32[]{:T(128)S(6)} %select_n.7), kind=kOutput, calls=%fused_computation.18 | convolution fusion | flops 3758096384 | bytes 19398660 | tf_op jit(solution)/shard_map/dot_general | solution.py:161
  70.7 5.6 maximum_bitcast_fusion.1
  76.4 106.8 %reduce-scatter.7.cloned.1.call-done = bf16[1,2,256,896]{2,3,1,0:T(8,128)(2,1)} async-done(((bf16[8,2,256,896]{2,3,1,0:T(8,128)(2,1)}), bf16[1,2,256,896]{2,3,1,0:T(8,128)(2,1)}) %reduce-scatter.7.cloned.1.call-update) | async-done | bytes 917520 | tf_op jit(solution)/shard_map/reduce_scatter | solution.py:145
  184.5 66.3 %reduce-scatter.9.cloned.1.call-done = f32[1,2,256,896]{2,3,1,0:T(8,128)} async-done(((f32[4,2,256,896]{2,3,1,0:T(8,128)}), f32[1,2,256,896]{2,3,1,0:T(8,128)}) %reduce-scatter.9.cloned.1.call-update) | async-done | bytes 1835024 | tf_op jit(solution)/shard_map/reduce_scatter | solution.py:145
  256.6 18.9 %all-gather.6.cloned.1.call-done.b_ref = bf16[3584,256]{1,0:T(8,128)(2,1)} async-done(((bf16[896,256]{1,0:T(8,128)(2,1)}), bf16[3584,256]{1,0:T(8,128)(2,1)}) %all-gather.6.cloned.1.call-update) | async-done | bytes 1835024 | tf_op jit(solution)/shard_map/all_gather | solution.py:147
  275.5 68.3 %all-gather.4.cloned.1.call-done.a_ref = bf16[7168,256]{1,0:T(8,128)(2,1)} async-done(((bf16[896,256]{1,0:T(8,128)(2,1)}), bf16[7168,256]{1,0:T(8,128)(2,1)}) %all-gather.4.cloned.1.call-update) | async-done | bytes 3670032 | tf_op jit(solution)/shard_map/all_gather | solution.py:147
  343.8 26.4 %make_kernel.1 = (bf16[7168,3584]{1,0:T(8,128)(2,1)}, f32[7168,1]{1,0:T(8,128)}) custom-call(bf16[7168,256]{1,0:T(8,128)(2,1)} %all-gather.4.cloned.1.call-done.a_ref, bf16[3584,256]{1,0:T(8,128)(2,1)} %all-gather.6.cloned.1.call-done.b_ref), custom_call_target="tpu_custom_call" | custom-call | flops 13153337344 | bytes 51380224 | tf_op jit(solution)/shard_map/make_kernel/pallas_call | solution.py:56
  373.3 34.9 %psum.42 = f32[7168]{0:T(1024)S(1)} all-reduce(f32[7168]{0:T(1024)S(1)} %reduce), channel_id=1, replica_groups=mesh['row'=4,'col'=8] {'col'}, use_global_device_ids=true, to_apply=%region_6.7 | all-reduce | flops 7168 | bytes 57344 | tf_op jit(solution)/shard_map/psum | solution.py:170
  412.3 22.9 %col_pass.3 = f32[1,3584]{1,0:T(1,128)} custom-call(bf16[7168,3584]{1,0:T(8,128)(2,1)} %get-tuple-element.7.k_ref, f32[7168,128]{1,0:T(8,128)} %broadcast_in_dim.6.r_ref), custom_call_target="tpu_custom_call" | custom-call | flops 51380224 | bytes 51380224 | tf_op jit(solution)/shard_map/col_pass/pallas_call | solution.py:124
  435.3 10.7 %psum.43 = f32[1,3584]{1,0:T(1,128)S(1)} all-reduce(f32[1,3584]{1,0:T(1,128)} %col_pass.3), channel_id=1, replica_groups=mesh['row'=4,'col'=8] {'row'}, use_global_device_ids=true, to_apply=%region_7.8 | all-reduce | flops 3584 | bytes 28672 | tf_op jit(solution)/shard_map/psum | solution.py:171
  446.6 27.8 %row_pass.2 = f32[7168,1]{1,0:T(8,128)} custom-call(bf16[7168,3584]{1,0:T(8,128)(2,1)} %get-tuple-element.7.k_ref, f32[1,3584]{1,0:T(1,128)} %broadcast_divide_fusion.4.c_ref), custom_call_target="tpu_custom_call" | custom-call | flops 51380224 | bytes 51380224 | tf_op jit(solution)/shard_map/row_pass/pallas_call | solution.py:95
  477.5 33.1 %psum.44 = f32[7168]{0:T(1024)S(1)} all-reduce(f32[7168]{0:T(1024)S(1)} %reduce.1), channel_id=1, replica_groups=mesh['row'=4,'col'=8] {'col'}, use_global_device_ids=true, to_apply=%region_8.9 | all-reduce | flops 7168 | bytes 57344 | tf_op jit(solution)/shard_map/psum | solution.py:170
  514.7 22.9 %col_pass.4 = f32[1,3584]{1,0:T(1,128)} custom-call(bf16[7168,3584]{1,0:T(8,128)(2,1)} %get-tuple-element.7.k_ref, f32[7168,128]{1,0:T(8,128)} %broadcast_in_dim.7.r_ref), custom_call_target="tpu_custom_call" | custom-call | flops 51380224 | bytes 51380224 | tf_op jit(solution)/shard_map/col_pass/pallas_call | solution.py:124
  537.7 10.7 %psum.45 = f32[1,3584]{1,0:T(1,128)S(1)} all-reduce(f32[1,3584]{1,0:T(1,128)} %col_pass.4), channel_id=1, replica_groups=mesh['row'=4,'col'=8] {'row'}, use_global_device_ids=true, to_apply=%region_9.10 | all-reduce | flops 3584 | bytes 28672 | tf_op jit(solution)/shard_map/psum | solution.py:171
  548.9 27.8 %row_pass.3 = f32[7168,1]{1,0:T(8,128)} custom-call(bf16[7168,3584]{1,0:T(8,128)(2,1)} %get-tuple-element.7.k_ref, f32[1,3584]{1,0:T(1,128)} %broadcast_divide_fusion.3.c_ref), custom_call_target="tpu_custom_call" | custom-call | flops 51380224 | bytes 51380224 | tf_op jit(solution)/shard_map/row_pass/pallas_call | solution.py:95
  579.8 33.3 %psum.46 = f32[7168]{0:T(1024)S(1)} all-reduce(f32[7168]{0:T(1024)S(1)} %reduce.2), channel_id=1, replica_groups=mesh['row'=4,'col'=8] {'col'}, use_global_device_ids=true, to_apply=%region_10.11 | all-reduce | flops 7168 | bytes 57344 | tf_op jit(solution)/shard_map/psum | solution.py:170
  617.3 22.9 %col_pass.5 = f32[1,3584]{1,0:T(1,128)} custom-call(bf16[7168,3584]{1,0:T(8,128)(2,1)} %get-tuple-element.7.k_ref, f32[7168,128]{1,0:T(8,128)} %broadcast_in_dim.8.r_ref), custom_call_target="tpu_custom_call" | custom-call | flops 51380224 | bytes 51380224 | tf_op jit(solution)/shard_map/col_pass/pallas_call | solution.py:124
  640.2 10.7 %psum.47 = f32[1,3584]{1,0:T(1,128)S(1)} all-reduce(f32[1,3584]{1,0:T(1,128)} %col_pass.5), channel_id=1, replica_groups=mesh['row'=4,'col'=8] {'row'}, use_global_device_ids=true, to_apply=%region_11.12 | all-reduce | flops 3584 | bytes 28672 | tf_op jit(solution)/shard_map/psum | solution.py:171
  658.2 22.3 %fusion = bf16[7168,256]{1,0:T(8,128)(2,1)} fusion(bf16[7168,3584]{1,0:T(8,128)(2,1)} %get-tuple-element.7.k_ref, f32[7168]{0:T(1024)S(1)} %broadcast_divide_fusion, bf16[3584,1024]{1,0:T(8,128)(2,1)S(1)} %multiply_convert_fusion), kind=kOutput, calls=%fused_computation.5 | convolution fusion | flops 13157007360 | bytes 56913920 | tf_op jit(solution)/shard_map/dot_general | solution.py:176
  680.6 23.3 %fusion.1 = bf16[7168,256]{1,0:T(8,128)(2,1)} fusion(bf16[7168,3584]{1,0:T(8,128)(2,1)} %get-tuple-element.7.k_ref, f32[7168]{0:T(1024)S(1)} %broadcast_divide_fusion, bf16[3584,1024]{1,0:T(8,128)(2,1)} %copy-done), kind=kOutput, calls=%fused_computation.6 | convolution fusion | flops 13157007360 | bytes 56913920 | tf_op jit(solution)/shard_map/dot_general | solution.py:176
  704.3 23.2 %fusion.2 = bf16[7168,256]{1,0:T(8,128)(2,1)} fusion(bf16[7168,3584]{1,0:T(8,128)(2,1)} %get-tuple-element.7.k_ref, f32[7168]{0:T(1024)S(1)} %broadcast_divide_fusion, bf16[3584,1024]{1,0:T(8,128)(2,1)} %copy-done), kind=kOutput, calls=%fused_computation.7 | convolution fusion | flops 13157007360 | bytes 56913920 | tf_op jit(solution)/shard_map/dot_general | solution.py:176
  727.6 23.1 %fusion.3 = bf16[7168,256]{1,0:T(8,128)(2,1)} fusion(bf16[7168,3584]{1,0:T(8,128)(2,1)} %get-tuple-element.7.k_ref, f32[7168]{0:T(1024)S(1)} %broadcast_divide_fusion, bf16[3584,1024]{1,0:T(8,128)(2,1)} %copy-done), kind=kOutput, calls=%fused_computation.8 | convolution fusion | flops 13157007360 | bytes 56913920 | tf_op jit(solution)/shard_map/dot_general | solution.py:176
  750.7 8.6 reduce-scatter.11.cloned.1.call-done
  759.2 84.3 %reduce-scatter.13.cloned.1.call-done = bf16[896,256]{1,0:T(8,128)(2,1)} async-done(((bf16[7168,256]{1,0:T(8,128)(2,1)}), bf16[896,256]{1,0:T(8,128)(2,1)}) %reduce-scatter.13.cloned.1.call-update) | async-done | bytes 458768 | tf_op jit(solution)/shard_map/reduce_scatter | solution.py:178
  843.6 84.4 %reduce-scatter.15.cloned.1.call-done = bf16[896,256]{1,0:T(8,128)(2,1)} async-done(((bf16[7168,256]{1,0:T(8,128)(2,1)}), bf16[896,256]{1,0:T(8,128)(2,1)}) %reduce-scatter.15.cloned.1.call-update) | async-done | bytes 458768 | tf_op jit(solution)/shard_map/reduce_scatter | solution.py:178
  928.0 84.3 %reduce-scatter.17.cloned.1.call-done = bf16[896,256]{1,0:T(8,128)(2,1)} async-done(((bf16[7168,256]{1,0:T(8,128)(2,1)}), bf16[896,256]{1,0:T(8,128)(2,1)}) %reduce-scatter.17.cloned.1.call-update) | async-done | bytes 458768 | tf_op jit(solution)/shard_map/reduce_scatter | solution.py:178
  (47 shorter events, 41.7 us)
Async XLA Ops:
  6.5 176.7 %reduce-scatter.7.cloned.1.call-start = ((), (), s32[]{:S(2)}) async-start(), calls=%async_computation.6 | async-start | bytes 8257536 | tf_op jit(solution)/shard_map/reduce_scatter | solution.py:145
  47.5 203.4 %reduce-scatter.9.cloned.1.call-start = ((), (), s32[]{:S(2)}) async-start(), calls=%async_computation.8 | async-start | bytes 9175040 | tf_op jit(solution)/shard_map/reduce_scatter | solution.py:145
  76.4 199.2 %all-gather.6.cloned.1.call-start = ((), (), s32[]{:S(2)}) async-start(), calls=%async_computation.9 | async-start | bytes 2293760 | tf_op jit(solution)/shard_map/all_gather | solution.py:147
  254.3 89.5 %all-gather.4.cloned.1.call-start = ((), (), s32[]{:S(2)}) async-start(), calls=%async_computation.7 | async-start | bytes 4128768 | tf_op jit(solution)/shard_map/all_gather | solution.py:147
  255.8 395.2 %all-gather.8.cloned.1.call-start = ((), (), s32[]{:S(2)}) async-start(), calls=%async_computation.10 | async-start | bytes 9175040 | tf_op jit(solution)/shard_map/all_gather | solution.py:164
  256.4 502.8 %reduce-scatter.11.cloned.1.call-start = ((), (), s32[]{:S(2)}) async-start(), calls=%async_computation.11 | async-start | bytes 4128768 | tf_op jit(solution)/shard_map/reduce_scatter | solution.py:178
  655.3 2.9 copy-start
  680.6 163.0 %reduce-scatter.13.cloned.1.call-start = ((), (), s32[]{:S(2)}) async-start(), calls=%async_computation.12 | async-start | bytes 4128768 | tf_op jit(solution)/shard_map/reduce_scatter | solution.py:178
  704.0 224.0 %reduce-scatter.15.cloned.1.call-start = ((), (), s32[]{:S(2)}) async-start(), calls=%async_computation.13 | async-start | bytes 4128768 | tf_op jit(solution)/shard_map/reduce_scatter | solution.py:178
  727.5 284.8 %reduce-scatter.17.cloned.1.call-start = ((), (), s32[]{:S(2)}) async-start(), calls=%async_computation.14 | async-start | bytes 4128768 | tf_op jit(solution)/shard_map/reduce_scatter | solution.py:178
  750.6 261.7 %copy-start.1 = (bf16[896,1024]{1,0:T(8,128)(2,1)S(1)}, bf16[896,1024]{1,0:T(8,128)(2,1)}, u32[]{:S(2)}) copy-start(bf16[896,1024]{1,0:T(8,128)(2,1)} %param.12) | copy-start | bytes 5505028
Sparse Core Ops, SparseCore 0:
  47.6 135.5 reduce-scatter.6
  185.7 65.0 reduce-scatter.8
  254.4 21.0 all-gather.5
  277.6 66.1 all-gather.3
  345.2 51.9 all-gather.7
  680.7 78.5 reduce-scatter.10
  762.9 80.6 reduce-scatter.12
  847.2 80.6 reduce-scatter.14
  931.6 80.6 reduce-scatter.16
